TPU v7x, 128 devices: a whole 4x4x4 slice. The times are simulated.
128 devices in a mesh: row: 8 (over x, core), col: 16 (over y, z).
Axes of the slice: x: 4, y: 4, z: 4, core: 2. Of those that a mesh axis runs over, the one named last changes fastest.
Arguments:
- features: bfloat16 [65536, 1024], P(('row', 'col')), may hold values from -6 to 6
- neighbours: int32 [65536, 16], P(('row', 'col')), may hold values from 0 to 3583, as said below
- degrees: int32 [65536], P(('row', 'col')), may hold values from 1 to 16, as said below
- send_rows: int32 [128, 2048], P(('row', 'col')), may hold values from 0 to 511
- send_count: int32 [128, 128], P(('row', 'col')), may hold values from 8 to 16, as said below
- hub_rows: int32 [1024], P(('row', 'col')), may hold values from 0 to 511, as said below
- w_self: bfloat16 [1024, 1024], replicated, may hold values from -0.1875 to 0.1875
- w_neigh: bfloat16 [1024, 1024], replicated, may hold values from -0.1875 to 0.1875
- bias_term: float32 [1024], replicated, may hold values from -3 to 3
- cotangent: bfloat16 [65536, 1024], P(('row', 'col')), may hold values from -6 to 6
Outputs:
- hidden: bfloat16 [65536, 1024], P(('row', 'col'))
- grad_x: bfloat16 [65536, 1024], P(('row', 'col'))
- grad_self: bfloat16 [1024, 1024], replicated
- grad_neigh: bfloat16 [1024, 1024], replicated
Inputs may be any that keep to these rules, and one draw needn't show every extreme that they name: neighbours of partition d point to its own rows (below 512), to live slots of arrived_d only (row 512 + p * 16 + s with p != d and s < send_count[p, d]), or to hub rows; entries at j >= degrees[i] also lie in the table. `degrees`: every seed has at least one neighbour. `send_count`: each partition sends between 8 and 16 live rows to each partition, and exactly 16 to the next one. `hub_rows`: the 8 hub rows of a partition are distinct.
All inputs are finite; a program needn't handle non-finite values.
Results may differ from a plain program's by a relative error of at most 0.0064.
Values may be sent and summed in bfloat16 or wider, within the bound.
A program may use at most 128 MiB of HBM per device.

v0:
```python
import jax
import jax.numpy as jnp
from jax import lax
from jax.sharding import PartitionSpec as P


def silu_slope(pre_act):
    sigmoid_val = jax.nn.sigmoid(pre_act)
    return sigmoid_val * (1.0 + pre_act * (1.0 - sigmoid_val))


def on_device(
    features,
    neighbours,
    degrees,
    send_rows,
    send_count,
    hub_rows,
    w_self,
    w_neigh,
    bias_term,
    cotangent,
):
    n_row = lax.axis_size("row")
    n_col = lax.axis_size("col")
    n_dev = n_row * n_col
    n_local, feat_width = features.shape
    fanout = neighbours.shape[1]
    capacity = send_rows.shape[1] // n_dev
    tile_size = min(512, n_local)
    n_tiles = n_local // tile_size
    slot_live = (
        jnp.arange(capacity, dtype=jnp.int32)[None, :] < send_count.reshape(n_dev, 1)
    ).reshape(-1, 1)
    outgoing = jnp.where(slot_live, features[send_rows[0]], jnp.zeros((), jnp.bfloat16))
    arrived = lax.all_to_all(outgoing, ("row", "col"), split_axis=0, concat_axis=0, tiled=True)
    own_hubs = features[hub_rows]
    all_hubs = lax.all_gather(own_hubs, ("row", "col"), axis=0, tiled=True)
    src_table = jnp.concatenate([features, arrived, all_hubs], 0)
    table_len = src_table.shape[0]
    live_mask = jnp.arange(fanout, dtype=jnp.int32)[None, :] < degrees[:, None]
    inv_deg = 1.0 / degrees.astype(jnp.float32)

    def gather_tile(tile_index):
        tile_live = live_mask.astype(jnp.bfloat16)
        picked = src_table[neighbours]
        return jnp.einsum("nf,nfd->nd", tile_live, picked, preferred_element_type=jnp.float32)

    summed = lax.map(gather_tile, jnp.arange(n_tiles, dtype=jnp.int32)).reshape(n_local, feat_width)
    aggregate = (summed * inv_deg[:, None]).astype(jnp.bfloat16)
    pre_act = (
        jnp.dot(features, w_self, preferred_element_type=jnp.float32)
        + jnp.dot(aggregate, w_neigh, preferred_element_type=jnp.float32)
        + bias_term[None, :]
    )
    hidden = jax.nn.silu(pre_act).astype(jnp.bfloat16)
    d_pre = (cotangent.astype(jnp.float32) * silu_slope(pre_act)).astype(jnp.bfloat16)
    self_part = lax.dot_general(
        features, d_pre, (((0,), (0,)), ((), ())), preferred_element_type=jnp.float32
    )
    neigh_part = lax.dot_general(
        aggregate, d_pre, (((0,), (0,)), ((), ())), preferred_element_type=jnp.float32
    )
    grad_self, grad_neigh = lax.psum((self_part, neigh_part), ("row", "col"))
    d_agg = (
        lax.dot_general(
            d_pre, w_neigh, (((1,), (1,)), ((), ())), preferred_element_type=jnp.float32
        )
        * inv_deg[:, None]
    )
    d_own = lax.dot_general(
        d_pre, w_self, (((1,), (1,)), ((), ())), preferred_element_type=jnp.float32
    )

    def spread_tile(tile_index, d_table):
        target = jnp.where(live_mask, neighbours, table_len)
        updates = jnp.broadcast_to(d_agg[:, None, :], (tile_size, fanout, feat_width))
        return d_table.at[target.reshape(-1)].add(updates.reshape(-1, feat_width), mode="drop")

    d_table = lax.fori_loop(
        0, n_tiles, spread_tile, jnp.zeros((table_len, feat_width), jnp.float32)
    )
    n_slots = n_dev * capacity
    d_local = d_table[:n_local]
    d_arrived = d_table[n_local : n_local + n_slots]
    d_hubs = d_table[n_local + n_slots :]
    returned = lax.all_to_all(
        d_arrived.astype(jnp.bfloat16), ("row", "col"), split_axis=0, concat_axis=0, tiled=True
    ).astype(d_arrived.dtype)
    hub_back = lax.psum_scatter(d_hubs, ("row", "col"), scatter_dimension=0, tiled=True)
    grad_x = d_own + d_local
    grad_x = grad_x.at[send_rows[0]].add(jnp.where(slot_live, returned, 0.0))
    grad_x = grad_x.at[hub_rows].add(hub_back)
    return (
        hidden,
        grad_x.astype(jnp.bfloat16),
        grad_self.astype(jnp.bfloat16),
        grad_neigh.astype(jnp.bfloat16),
    )


def solution(mesh):
    in_specs = (
        P(("row", "col"), None),
        P(("row", "col"), None),
        P(("row", "col")),
        P(("row", "col"), None),
        P(("row", "col"), None),
        P(("row", "col")),
        P(),
        P(),
        P(),
        P(("row", "col"), None),
    )
    out_specs = (P(("row", "col"), None), P(("row", "col"), None), P(), P())
    return jax.shard_map(
        on_device, mesh=mesh, in_specs=in_specs, out_specs=out_specs, check_vma=False
    )
```

profile of v0, /device:TPU:0, one launch (start us, length us, event | category | flops | bytes accessed | tf_op | source)
XLA Modules:
  0.0 957.6 jit_solution(10110251208233370689)
XLA Ops:
  7.2 0.0 copy-start
  7.2 0.0 all-gather.3.cloned.1.call-start
  7.2 0.8 compare_select_fusion.3
  8.0 2.5 gather_fusion.1
  10.6 0.0 all-gather.3.cloned.1.call-update
  10.6 0.7 compare_select_fusion.2
  11.3 0.0 copy-start.9
  11.3 12.3 %gather_fusion = bf16[2048,1024]{1,0:T(8,128)(2,1)} fusion(bf16[512,1024]{1,0:T(8,128)(2,1)} %param.10, s32[2048]{0:T(1024)S(1)} %broadcast_clamp_fusion.1), kind=kCustom, calls=%fused_computation | custom fusion | bytes 8396800 | tf_op jit(solution)/shard_map/gather | solution.py:35
  23.7 0.0 copy-done.9
  23.7 0.1 iota_compare_fusion
  23.8 3.8 broadcast_select_fusion
  27.6 11.7 %all-to-all-start = ((bf16[128,16,1024]{2,1,0:T(8,128)(2,1)}), bf16[128,16,1024]{2,1,0:T(8,128)(2,1)}, u32[]{:S(2)}, u32[]{:S(2)}) async-start(bf16[128,16,1024]{2,1,0:T(8,128)(2,1)} %broadcast_select_fusion), calls=%async_computation | async-start | bytes 8388608 | tf_op jit(solution)/shard_map/all_to_all | solution.py:36
  39.3 0.0 reduce-scatter.2.cloned.1.call-start
  39.3 0.0 copy-done.8
  39.4 0.4 copy.18
  39.8 0.0 copy-done.7
  39.8 0.8 copy.15
  40.7 1.1 reshape.128
  41.8 0.8 copy.16
  42.6 1.1 reshape.107
  43.7 0.0 copy-done.1
  43.7 4.2 fusion.11
  48.0 64.1 %all-gather.3.cloned.1.call-done = bf16[1024,1024]{1,0:T(8,128)(2,1)} async-done(((bf16[8,1024]{1,0:T(8,128)(2,1)}), bf16[1024,1024]{1,0:T(8,128)(2,1)}) %all-gather.3.cloned.1.call-update) | async-done | bytes 2097168 | tf_op jit(solution)/shard_map/all_gather | solution.py:38
  112.1 0.0 all-to-all-done
  112.1 6.3 pad_maximum_fusion
  118.3 44.7 %gather_fusion.2 = bf16[8192,1024]{1,0:T(8,128)(2,1)} fusion(bf16[3584,1024]{1,0:T(8,128)(2,1)} %pad_maximum_fusion, s32[8192]{0:T(1024)S(1)} %broadcast_clamp_fusion), kind=kCustom, calls=%fused_computation.2 | custom fusion | bytes 33587200 | tf_op jit(solution)/shard_map/while/body/eval_jaxpr/gather | solution.py:46
  163.0 8.6 fusion.12
  171.7 0.0 copy-start.2
  171.7 3.0 multiply_convert_fusion
  174.7 1.3 convolution_multiply_fusion
  176.1 11.3 %broadcast_in_dim.67 = f32[512,16,1024]{2,1,0:T(8,128)} broadcast(f32[512,1024]{1,0:T(8,128)S(1)} %convolution_multiply_fusion), dimensions={0,2} | broadcast | bytes 35651584 | tf_op jit(solution)/shard_map/while/body/eval_jaxpr/broadcast_in_dim | solution.py:77
  187.4 77.1 %scatter_custom_fusion = f32[3584,1024]{1,0:T(8,128)} fusion(s32[8192]{0:T(1024)S(1)} %bitcast.40, f32[8192,1024]{1,0:T(8,128)} %bitcast.37, f32[]{:T(128)} %constant.13.clone.1), kind=kCustom, calls=%fused_computation.10 | custom fusion | flops 8388608 | bytes 14680576 | tf_op jit(solution)/shard_map/while/body/eval_jaxpr/scatter-add | solution.py:78
  264.4 4.7 slice.21
  269.2 0.0 reduce-scatter.2.cloned.1.call-update
  269.2 6.0 slice.24
  275.2 6.6 all-to-all-start.1
  281.8 0.1 lt.79
  281.9 0.0 copy-start.5
  281.9 4.6 convolution_bitcast_fusion
  286.5 3.5 fusion.8
  290.1 147.6 %all-reduce.2 = (bf16[1024,1024]{0,1:T(8,128)(2,1)}, bf16[1024,1024]{1,0:T(8,128)(2,1)}) all-reduce(f32[1024,1024]{0,1:T(8,128)} %convolution_bitcast_fusion, f32[1024,1024]{1,0:T(8,128)} %fusion.8), channel_id=1, replica_groups=mesh['row'=8,'col'=16] {'row','col'}, use_global_device_ids=true, to_apply=%region_4.5 | all-reduce | flops 2097152 | bytes 12582912 | tf_op jit(solution)/shard_map/psum | solution.py:64
  437.7 4.0 copy.17
  441.7 4.9 slice_add_fusion
  446.6 0.0 all-to-all-done.1
  446.6 21.7 %scatter_custom_fusion.1 = f32[512,1024]{1,0:T(8,128)} fusion(f32[512,1024]{1,0:T(8,128)} %slice_add_fusion, s32[2048]{0:T(1024)S(1)} %bitcast.42, bf16[2048,1024]{1,0:T(8,128)(2,1)} %bitcast.13, f32[]{:T(128)} %constant.13.clone.1, pred[2048]{0:T(1024)(128)(4,1)S(1)} %lt.79), kind=kCustom, calls=%fused_computation.8 | custom fusion | flops 6291456 | bytes 6294016 | tf_op jit(solution)/shard_map/scatter-add | solution.py:92
  468.3 476.0 %reduce-scatter.2.cloned.1.call-done = f32[8,1024]{1,0:T(8,128)} async-done(((f32[1024,1024]{1,0:T(8,128)}), f32[8,1024]{1,0:T(8,128)}) %reduce-scatter.2.cloned.1.call-update) | async-done | bytes 32784 | tf_op jit(solution)/shard_map/reduce_scatter | solution.py:90
  944.3 3.7 scatter_fusion
  948.0 2.7 convert_element_type.40
  (25 shorter events, 0.1 us)
Async XLA Ops:
  7.2 164.5 %copy-start = (bf16[1024,1024]{1,0:T(8,128)(2,1)S(1)}, bf16[1024,1024]{1,0:T(8,128)(2,1)}, u32[]{:S(2)}) copy-start(bf16[1024,1024]{1,0:T(8,128)(2,1)} %param.17) | copy-start | bytes 6291460
  7.2 104.9 %all-gather.3.cloned.1.call-start = ((), (), s32[]{:S(2)}) async-start(), calls=%async_computation.4 | async-start | bytes 2113536 | tf_op jit(solution)/shard_map/all_gather | solution.py:38
  11.3 12.3 %copy-start.9 = (s32[1,128]{1,0:T(1,128)S(1)}, s32[1,128]{1,0:T(1,128)}, u32[]{:S(2)}) copy-start(s32[1,128]{1,0:T(1,128)} %param.14) | copy-start | bytes 1540
  27.6 11.8 %copy-start.8 = (s32[512]{0:T(512)S(1)}, s32[512]{0:T(512)}, u32[]{:S(2)}) copy-start(s32[512]{0:T(512)} %param.12) | copy-start | bytes 6148
  27.6 12.2 %copy-start.7 = (s32[512,16]{0,1:T(8,128)S(1)}, s32[512,16]{0,1:T(8,128)}, u32[]{:S(2)}) copy-start(s32[512,16]{0,1:T(8,128)} %param.11) | copy-start | bytes 98308
  27.6 16.1 %copy-start.1 = (bf16[512,1024]{1,0:T(8,128)(2,1)S(1)}, bf16[512,1024]{1,0:T(8,128)(2,1)}, u32[]{:S(2)}) copy-start(bf16[512,1024]{1,0:T(8,128)(2,1)} %param.10) | copy-start | bytes 3145732
  27.6 84.5 %all-to-all-start = ((bf16[128,16,1024]{2,1,0:T(8,128)(2,1)}), bf16[128,16,1024]{2,1,0:T(8,128)(2,1)}, u32[]{:S(2)}, u32[]{:S(2)}) async-start(bf16[128,16,1024]{2,1,0:T(8,128)(2,1)} %broadcast_select_fusion), calls=%async_computation | async-start | bytes 8388608 | tf_op jit(solution)/shard_map/all_to_all | solution.py:36
  39.3 905.0 %reduce-scatter.2.cloned.1.call-start = ((), (), s32[]{:S(2)}) async-start(), calls=%async_computation.3 | async-start | bytes 4227072 | tf_op jit(solution)/shard_map/reduce_scatter | solution.py:90
  163.0 8.7 copy-start.10
  163.0 8.7 copy-start.11
  163.0 8.7 copy-start.12
  171.7 3.1 copy-start.2
  174.7 1.3 copy-start.4
  275.2 171.4 %all-to-all-start.1 = ((bf16[128,16,1024]{2,1,0:T(8,128)(2,1)}), bf16[128,16,1024]{2,1,0:T(8,128)(2,1)}, u32[]{:S(2)}, u32[]{:S(2)}) async-start(bf16[128,16,1024]{2,1,0:T(8,128)(2,1)} %bitcast.39), calls=%async_computation.1 | async-start | bytes 8388608 | tf_op jit(solution)/shard_map/all_to_all | solution.py:87
  281.9 4.6 copy-start.3
  281.9 4.6 copy-start.5
  437.7 4.0 copy-start.6
Sparse Core Ops, SparseCore 0:
  11.5 100.4 all-gather.2
  269.3 674.8 reduce-scatter.1
where the time goes:
time: 959 us; the launch traced here: 958 us
  waiting for transfers between devices  540 us (56%)
  blocking collectives  148 us (15%)
  other arithmetic  117 us (12%)
  local copies, waits for them, and re-layouts  90.1 us (9%)
  matrix products  30.2 us (3%)
  starting transfers between devices  18.4 us (2%)
  between operations  14.3 us (1%)
    reduce_scatter x1, waiting for transfers between devices, on_device(): lax.psum_scatter(d_hubs, ('row', 'col'), scatter_dimension=0, tiled=True)  476 us
    psum x1, blocking collectives, on_device(): grad_self, grad_neigh = lax.psum((self_part, neigh_part), ('row', 'col'))  148 us
    scatter-add x1, other arithmetic, spread_tile(): d_table.at[target.reshape(-1)]  77.1 us
    all_gather x1, waiting for transfers between devices, on_device(): all_hubs = lax.all_gather(own_hubs, ('row', 'col'), axis=0, tiled=True)  64.1 us
    gather x1, local copies, waits for them, and re-layouts, gather_tile(): picked = src_table[neighbours]  44.7 us
    scatter-add x1, other arithmetic, on_device(): grad_x = grad_x.at[send_rows[0]].add(jnp.where(slot_live, returned, 0.0))  21.7 us
  transfers between devices with their start and end apart: 4, of which 2 were waited for; matrix products, arithmetic and copies ran while one was open for 7% of the time, Pallas kernels for 0%

commit v1 on v0

--- a/solution.py
+++ b/solution.py
@@ -61,7 +61,7 @@
     neigh_part = lax.dot_general(
         aggregate, d_pre, (((0,), (0,)), ((), ())), preferred_element_type=jnp.float32
     )
-    grad_self, grad_neigh = lax.psum((self_part, neigh_part), ("row", "col"))
+    grad_self, grad_neigh = lax.psum(lax.psum((self_part, neigh_part), "row"), "col")
     d_agg = (
         lax.dot_general(
             d_pre, w_neigh, (((1,), (1,)), ((), ())), preferred_element_type=jnp.float32

time: 959 us -> 979 us (1.021)
  blocking collectives: 148 us -> 203 us
  waiting for transfers between devices: 540 us -> 507 us
    reduce_scatter x1, waiting for transfers between devices: 476 us -> 393 us  [on_device(): lax.psum_scatter(d_hubs, ('row', 'col'), scatter_dimension=0, tiled=True)]
    psum x1, blocking collectives: 148 us -> 203 us  [on_device(): lax.psum(lax.psum((self_part, neigh_part), 'row'), 'col')]
    all_to_all x1, waiting for transfers between devices: 0.01 us -> 47.2 us  [on_device(): lax.all_to_all(d_arrived.astype(jnp.bfloat16), ('row', 'col'), split_axis...]
  transfers between devices with their start and end apart: 4 -> 5, of which waited for: 2 -> 3; matrix products, arithmetic and copies ran while one was open for 7% -> 16% of each run, Pallas kernels for 0% -> 0%
where the time goes in v1:
time: 979 us; the launch traced here: 978 us
  waiting for transfers between devices  507 us (52%)
  blocking collectives  203 us (21%)
  other arithmetic  117 us (12%)
  local copies, waits for them, and re-layouts  89.6 us (9%)
  matrix products  28.9 us (3%)
  starting transfers between devices  18.8 us (2%)
  between operations  13.9 us (1%)
    reduce_scatter x1, waiting for transfers between devices, on_device(): lax.psum_scatter(d_hubs, ('row', 'col'), scatter_dimension=0, tiled=True)  393 us
    psum x1, blocking collectives, on_device(): lax.psum(lax.psum((self_part, neigh_part), 'row'), 'col')  203 us
    scatter-add x1, other arithmetic, spread_tile(): d_table.at[target.reshape(-1)]  77.1 us
    all_gather x1, waiting for transfers between devices, on_device(): all_hubs = lax.all_gather(own_hubs, ('row', 'col'), axis=0, tiled=True)  66.1 us
    all_to_all x1, waiting for transfers between devices, on_device(): lax.all_to_all(d_arrived.astype(jnp.bfloat16), ('row', 'col'), split_axis...  47.2 us
    gather x1, local copies, waits for them, and re-layouts, gather_tile(): picked = src_table[neighbours]  44.7 us
    scatter-add x1, other arithmetic, on_device(): grad_x = grad_x.at[send_rows[0]].add(jnp.where(slot_live, returned, 0.0))  21.7 us
  transfers between devices with their start and end apart: 5, of which 3 were waited for; matrix products, arithmetic and copies ran while one was open for 16% of the time, Pallas kernels for 0%

profile of v1, /device:TPU:0, one launch (start us, length us, event | category | flops | bytes accessed | tf_op | source)
XLA Modules:
  0.0 977.7 jit_solution(722586127917534417)
XLA Ops:
  7.2 0.0 copy-start
  7.2 0.0 all-gather.3.cloned.1.call-start
  7.2 0.8 compare_select_fusion.3
  8.0 2.5 gather_fusion.1
  10.6 0.0 all-gather.3.cloned.1.call-update
  10.6 0.7 compare_select_fusion.2
  11.3 0.0 copy-start.6
  11.3 12.3 %gather_fusion = bf16[2048,1024]{1,0:T(8,128)(2,1)} fusion(bf16[512,1024]{1,0:T(8,128)(2,1)} %param.10, s32[2048]{0:T(1024)S(1)} %broadcast_clamp_fusion.1), kind=kCustom, calls=%fused_computation | custom fusion | bytes 8396800 | tf_op jit(solution)/shard_map/gather | solution.py:35
  23.7 0.0 copy-done.6
  23.7 0.1 iota_compare_fusion
  23.8 3.8 broadcast_select_fusion
  27.6 11.7 %all-to-all-start = ((bf16[128,16,1024]{2,1,0:T(8,128)(2,1)}), bf16[128,16,1024]{2,1,0:T(8,128)(2,1)}, u32[]{:S(2)}, u32[]{:S(2)}) async-start(bf16[128,16,1024]{2,1,0:T(8,128)(2,1)} %broadcast_select_fusion), calls=%async_computation | async-start | bytes 8388608 | tf_op jit(solution)/shard_map/all_to_all | solution.py:36
  39.3 0.0 all-reduce.5.cloned.1.call-start
  39.3 0.0 copy-done.5
  39.4 0.4 copy.18
  39.8 0.0 copy-done.4
  39.8 0.8 copy.15
  40.7 1.1 reshape.128
  41.8 4.2 fusion.11
  46.0 66.1 %all-gather.3.cloned.1.call-done = bf16[1024,1024]{1,0:T(8,128)(2,1)} async-done(((bf16[8,1024]{1,0:T(8,128)(2,1)}), bf16[1024,1024]{1,0:T(8,128)(2,1)}) %all-gather.3.cloned.1.call-update) | async-done | bytes 2097168 | tf_op jit(solution)/shard_map/all_gather | solution.py:38
  112.1 0.0 all-to-all-done
  112.1 6.3 pad_maximum_fusion
  118.3 44.7 %gather_fusion.2 = bf16[8192,1024]{1,0:T(8,128)(2,1)} fusion(bf16[3584,1024]{1,0:T(8,128)(2,1)} %pad_maximum_fusion, s32[8192]{0:T(1024)S(1)} %broadcast_clamp_fusion), kind=kCustom, calls=%fused_computation.2 | custom fusion | bytes 33587200 | tf_op jit(solution)/shard_map/while/body/eval_jaxpr/gather | solution.py:46
  163.0 8.6 fusion.12
  171.7 3.0 multiply_convert_fusion
  174.7 3.3 convolution_bitcast_fusion
  178.0 3.7 fusion.8
  181.7 0.0 all-reduce.5.cloned.1.call-update
  181.7 0.2 reduce-scatter.2.cloned.1.call-start
  182.0 0.1 copy.16
  182.1 0.2 reshape.107
  182.3 0.6 copy-done.3
  182.9 1.3 convolution_multiply_fusion
  184.2 11.8 %broadcast_in_dim.67 = f32[512,16,1024]{2,1,0:T(8,128)} broadcast(f32[512,1024]{1,0:T(8,128)S(1)} %convolution_multiply_fusion), dimensions={0,2} | broadcast | bytes 35651584 | tf_op jit(solution)/shard_map/while/body/eval_jaxpr/broadcast_in_dim | solution.py:77
  196.1 77.1 %scatter_custom_fusion = f32[3584,1024]{1,0:T(8,128)} fusion(s32[8192]{0:T(1024)S(1)} %bitcast.40, f32[8192,1024]{1,0:T(8,128)} %bitcast.37, f32[]{:T(128)} %constant.13.clone.1), kind=kCustom, calls=%fused_computation.10 | custom fusion | flops 8388608 | bytes 14680576 | tf_op jit(solution)/shard_map/while/body/eval_jaxpr/scatter-add | solution.py:78
  273.2 4.8 slice.21
  278.0 0.0 reduce-scatter.2.cloned.1.call-update
  278.0 6.0 slice.24
  284.1 6.8 all-to-all-start.1
  290.9 0.1 lt.79
  291.0 4.8 slice_add_fusion
  295.8 47.2 %all-to-all-done.1 = bf16[128,16,1024]{2,1,0:T(8,128)(2,1)} async-done(((bf16[128,16,1024]{2,1,0:T(8,128)(2,1)}), bf16[128,16,1024]{2,1,0:T(8,128)(2,1)}, u32[]{:S(2)}, u32[]{:S(2)}) %all-to-all-start.1) | async-done | bytes 4194336 | tf_op jit(solution)/shard_map/all_to_all | solution.py:87
  343.0 21.7 %scatter_custom_fusion.1 = f32[512,1024]{1,0:T(8,128)} fusion(f32[512,1024]{1,0:T(8,128)} %slice_add_fusion, s32[2048]{0:T(1024)S(1)} %bitcast.42, bf16[2048,1024]{1,0:T(8,128)(2,1)} %bitcast.13, f32[]{:T(128)} %constant.13.clone.1, pred[2048]{0:T(1024)(128)(4,1)S(1)} %lt.79), kind=kCustom, calls=%fused_computation.8 | custom fusion | flops 6291456 | bytes 6294016 | tf_op jit(solution)/shard_map/scatter-add | solution.py:92
  364.7 202.7 %all-reduce.6 = (bf16[1024,1024]{0,1:T(8,128)(2,1)}, bf16[1024,1024]{1,0:T(8,128)(2,1)}) all-reduce(f32[1024,1024]{0,1:T(8,128)} %get-tuple-element.44, f32[1024,1024]{1,0:T(8,128)} %get-tuple-element.45), channel_id=1, replica_groups=mesh['row'=8,'col'=16] {'col'}, use_global_device_ids=true, to_apply=%region_5.6 | all-reduce | flops 2097152 | bytes 12582912 | tf_op jit(solution)/shard_map/psum | solution.py:64
  567.4 3.9 copy.17
  571.3 393.4 %reduce-scatter.2.cloned.1.call-done = f32[8,1024]{1,0:T(8,128)} async-done(((f32[1024,1024]{1,0:T(8,128)}), f32[8,1024]{1,0:T(8,128)}) %reduce-scatter.2.cloned.1.call-update) | async-done | bytes 32784 | tf_op jit(solution)/shard_map/reduce_scatter | solution.py:90
  964.7 3.7 scatter_fusion
  968.5 2.7 convert_element_type.40
  (22 shorter events, 0.1 us)
Async XLA Ops:
  7.2 164.5 %copy-start = (bf16[1024,1024]{1,0:T(8,128)(2,1)S(1)}, bf16[1024,1024]{1,0:T(8,128)(2,1)}, u32[]{:S(2)}) copy-start(bf16[1024,1024]{1,0:T(8,128)(2,1)} %param.17) | copy-start | bytes 6291460
  7.2 104.9 %all-gather.3.cloned.1.call-start = ((), (), s32[]{:S(2)}) async-start(), calls=%async_computation.4 | async-start | bytes 2113536 | tf_op jit(solution)/shard_map/all_gather | solution.py:38
  11.3 12.3 %copy-start.6 = (s32[1,128]{1,0:T(1,128)S(1)}, s32[1,128]{1,0:T(1,128)}, u32[]{:S(2)}) copy-start(s32[1,128]{1,0:T(1,128)} %param.14) | copy-start | bytes 1540
  27.6 11.8 %copy-start.5 = (s32[512]{0:T(512)S(1)}, s32[512]{0:T(512)}, u32[]{:S(2)}) copy-start(s32[512]{0:T(512)} %param.12) | copy-start | bytes 6148
  27.6 12.2 %copy-start.4 = (s32[512,16]{0,1:T(8,128)S(1)}, s32[512,16]{0,1:T(8,128)}, u32[]{:S(2)}) copy-start(s32[512,16]{0,1:T(8,128)} %param.11) | copy-start | bytes 98308
  27.6 14.2 %copy-start.1 = (bf16[512,1024]{1,0:T(8,128)(2,1)S(1)}, bf16[512,1024]{1,0:T(8,128)(2,1)}, u32[]{:S(2)}) copy-start(bf16[512,1024]{1,0:T(8,128)(2,1)} %param.10) | copy-start | bytes 3145732
  27.6 84.5 %all-to-all-start = ((bf16[128,16,1024]{2,1,0:T(8,128)(2,1)}), bf16[128,16,1024]{2,1,0:T(8,128)(2,1)}, u32[]{:S(2)}, u32[]{:S(2)}) async-start(bf16[128,16,1024]{2,1,0:T(8,128)(2,1)} %broadcast_select_fusion), calls=%async_computation | async-start | bytes 8388608 | tf_op jit(solution)/shard_map/all_to_all | solution.py:36
  39.3 325.4 %all-reduce.5.cloned.1.call-start = ((), (), s32[]{:S(2)}) async-start(), calls=%async_computation.5 | async-start | bytes 16777216 | tf_op jit(solution)/shard_map/psum | solution.py:64
  163.0 8.7 copy-start.7
  163.0 8.7 copy-start.8
  163.0 8.7 copy-start.9
  174.7 3.3 copy-start.2
  181.7 1.2 copy-start.3
  181.7 783.0 %reduce-scatter.2.cloned.1.call-start = ((), (), s32[]{:S(2)}) async-start(), calls=%async_computation.3 | async-start | bytes 4227072 | tf_op jit(solution)/shard_map/reduce_scatter | solution.py:90
  284.1 59.0 %all-to-all-start.1 = ((bf16[128,16,1024]{2,1,0:T(8,128)(2,1)}), bf16[128,16,1024]{2,1,0:T(8,128)(2,1)}, u32[]{:S(2)}, u32[]{:S(2)}) async-start(bf16[128,16,1024]{2,1,0:T(8,128)(2,1)} %bitcast.39), calls=%async_computation.1 | async-start | bytes 8388608 | tf_op jit(solution)/shard_map/all_to_all | solution.py:87
Sparse Core Ops, SparseCore 0:
  11.5 100.4 all-gather.2
  181.9 101.2 all-reduce.4
  285.5 679.1 reduce-scatter.1
